TPU v7x, 256 devices: a whole 4x4x8 slice. The times are simulated.
256 devices in a mesh: probe: 4 (over x), space: 64 (over y, z, core).
Axes of the slice: x: 4, y: 4, z: 8, core: 2. Of those that a mesh axis runs over, the one named last changes fastest.
Arguments:
- courant_field: float32 [128, 32, 256], P('space'), may hold values from 0.05 to 0.3
- probe_fields: float32 [16, 128, 32, 256], P('probe', 'space'), may hold values from -6 to 6
- prior_weight: float32 [128, 32, 256], P('space'), may hold values from 0.5 to 5
- source_cells: int32 [4096], P('space'), may hold values from 0 to 1048575, as said below
- source_strength: float32 [4096], P('space'), may hold values from -6 to 6
- wavelet: float32 [8], replicated, may hold values from -4 to 4
- receiver_cells: int32 [4096], P('space'), may hold values from 0 to 1048575, as said below
- receiver_weight: float32 [4096], P('space'), may hold values from 1 to 10
Outputs:
- hessian_fields: float32 [16, 128, 32, 256], P('probe', 'space')
- basis: float32 [16, 128, 32, 256], P('probe', 'space')
Inputs may be any that keep to these rules, and one draw needn't show every extreme that they name: `source_cells`: entries k * 64 to (k + 1) * 64 - 1 are cells of the k-th slab of 2 planes along the first dimension; cells may repeat. `receiver_cells`: entries k * 64 to (k + 1) * 64 - 1 are cells of the k-th slab of 2 planes along the first dimension; cells may repeat.
All inputs are finite; a program needn't handle non-finite values.
Results may differ from a plain program's by a relative error of at most 0.0019.
Values sent between devices are 32-bit elements; how exact they have to be, the bound alone decides.
No kernel may reach another device: no remote copies, remote signals or barrier semaphores. Data moves between devices by JAX's collectives and lax.ppermute only.
A program may use at most 64 MiB of HBM per device.

v0:
```python
import jax
import jax.numpy as jnp
from jax import lax
from jax.sharding import PartitionSpec as P


def extended(block, sides, width):
    for axis, dim in sides:
        count = lax.axis_size(axis)
        forward = [(i, i + 1) for i in range(count - 1)]
        backward = [(target, source) for source, target in forward]
        low = lax.ppermute(
            lax.slice_in_dim(block, block.shape[dim] - width, None, axis=dim), axis, forward
        )
        high = lax.ppermute(lax.slice_in_dim(block, 0, width, axis=dim), axis, backward)
        block = jnp.concatenate([low, block, high], axis=dim)
    return block


def laplace_local(padded, center):
    side = jnp.pad(center, ((0, 0), (0, 0), (1, 1), (1, 1)))
    total = padded[:, 2:] + padded[:, :-2]
    total = total + side[:, :, 2:, 1:-1] + side[:, :, :-2, 1:-1]
    total = total + side[:, :, 1:-1, 2:] + side[:, :, 1:-1, :-2]
    return total - 6.0 * center


def inject(values, local_cells, field_shape):
    flat = jnp.zeros(
        (field_shape[0], field_shape[1] * field_shape[2] * field_shape[3]), jnp.float32
    )
    return flat.at[:, local_cells].add(values).reshape(field_shape)


def inner_rows(rows):
    return lax.dot_general(
        rows,
        rows,
        (((1,), (1,)), ((), ())),
        precision=lax.Precision.HIGHEST,
        preferred_element_type=jnp.float32,
    )


def shards(
    courant_field,
    probe_fields,
    prior_weight,
    source_cells,
    source_strength,
    wavelet,
    receiver_cells,
    receiver_weight,
):
    field_shape = probe_fields.shape
    groups = field_shape[0]
    cells = field_shape[1] * field_shape[2] * field_shape[3]
    steps_total = wavelet.shape[0]
    offset = lax.axis_index("space") * cells
    source_local = source_cells - offset
    receiver_local = receiver_cells - offset
    source_field = (
        jnp.zeros((cells,), jnp.float32)
        .at[source_local]
        .add(source_strength)
        .reshape(field_shape[1:])
    )
    state_prev = jnp.zeros((groups + 1,) + field_shape[1:], jnp.float32)
    state_now = jnp.concatenate(
        [(wavelet[0] * source_field)[None], jnp.zeros(field_shape, jnp.float32)], 0
    )
    drives = [None]
    records = [None]
    for step in range(1, steps_total):
        padded = extended(state_now, (("space", 1),), 1)
        bent = laplace_local(padded, state_now)
        drive = courant_field * bent[0]
        forcing = jnp.concatenate(
            [(wavelet[step] * source_field)[None], probe_fields * drive[None]], 0
        )
        state_next = 2.0 * state_now - state_prev + courant_field * bent + forcing
        drives.append(drive)
        records.append(jnp.take(state_next[1:].reshape(groups, cells), receiver_local, axis=1))
        state_prev, state_now = (state_now, state_next)
    adjoint_next = inject(receiver_weight * records[steps_total - 1], receiver_local, field_shape)
    adjoint_after = jnp.zeros(field_shape, jnp.float32)
    hessian = prior_weight * probe_fields + drives[steps_total - 1] * adjoint_next
    for level in range(steps_total - 1, 1, -1):
        scaled = courant_field * adjoint_next
        padded = extended(scaled, (("space", 1),), 1)
        injected = inject(receiver_weight * records[level - 1], receiver_local, field_shape)
        adjoint_now = 2.0 * adjoint_next - adjoint_after + laplace_local(padded, scaled) + injected
        hessian = hessian + drives[level - 1] * adjoint_now
        adjoint_after, adjoint_next = (adjoint_next, adjoint_now)
    flat = hessian.reshape(groups, cells)
    total_cells = cells * lax.axis_size("space")
    rows = lax.all_gather(flat, "probe", axis=0, tiled=True)
    gram = lax.psum(inner_rows(rows), "space") / total_cells
    lower = jnp.linalg.cholesky(gram)
    solved = lax.linalg.triangular_solve(lower, rows, left_side=True, lower=True)
    mine = lax.dynamic_slice_in_dim(solved, lax.axis_index("probe") * groups, groups, 0)
    return (hessian, mine.reshape(field_shape))


def solution(mesh):
    in_specs = (
        P("space", None, None),
        P("probe", "space", None, None),
        P("space", None, None),
        P("space"),
        P("space"),
        P(),
        P("space"),
        P("space"),
    )
    out_specs = (P("probe", "space", None, None), P("probe", "space", None, None))
    return jax.shard_map(shards, mesh=mesh, in_specs=in_specs, out_specs=out_specs, check_vma=False)
```

profile of v0, /device:TPU:4, one launch (start us, length us, event | category | flops | bytes accessed | tf_op | source)
XLA Modules:
  0.0 436.4 jit_solution(6910389396807057819)
XLA Ops:
  10.6 5.0 %broadcast_multiply_fusion.13 = (f32[16384]{0:T(1024)S(1)}, f32[16384]{0:T(1024)S(1)}, f32[16384]{0:T(1024)S(1)}, f32[16384]{0:T(1024)S(1)}, f32[16384]{0:T(1024...) fusion(f32[16384]{0:T(1024)S(1)} %scatter_custom_fusion, f32[]{:T(128)} %bitcast.14, f32[]{:T(128)} %bitcast.11, ...), kind=kLoop, calls=%fused_computation.264 | loop fusion | flops 131072 | bytes 589856 | tf_op jit(solution)/shard_map/mul | solution.py:79
  25.6 5.8 %collective-permute-start.3 = (f32[5,1,32,256]{3,2,1,0:T(8,128)S(1)}, f32[5,1,32,256]{3,2,1,0:T(8,128)S(1)}, u32[]{:S(2)}, u32[]{:S(2)}) collective-permute-start(f32[5,1,32,256]{3,2,1,0:T(8,128)S(1)} %get-tuple-element.29), channel_id=1, source_target_pairs={{0,1},{1,2},{2,3},{3,4},{4,5},{5,6},{6,7},{7,8},{8,9},{9,10},{10,1... | collective-permute-start | bytes 491528 | tf_op jit(solution)/shard_map/ppermute | solution.py:12
  37.9 5.6 %collective-permute-start.5 = (f32[5,1,32,256]{3,2,1,0:T(8,128)S(1)}, f32[5,1,32,256]{3,2,1,0:T(8,128)S(1)}, u32[]{:S(2)}, u32[]{:S(2)}) collective-permute-start(f32[5,1,32,256]{3,2,1,0:T(8,128)S(1)} %get-tuple-element.27), channel_id=1, source_target_pairs={{0,1},{1,2},{2,3},{3,4},{4,5},{5,6},{6,7},{7,8},{8,9},{9,10},{10,1... | collective-permute-start | bytes 491528 | tf_op jit(solution)/shard_map/ppermute | solution.py:12
  47.4 5.6 %collective-permute-start.7 = (f32[5,1,32,256]{3,2,1,0:T(8,128)S(1)}, f32[5,1,32,256]{3,2,1,0:T(8,128)S(1)}, u32[]{:S(2)}, u32[]{:S(2)}) collective-permute-start(f32[5,1,32,256]{3,2,1,0:T(8,128)S(1)} %get-tuple-element.25), channel_id=1, source_target_pairs={{0,1},{1,2},{2,3},{3,4},{4,5},{5,6},{6,7},{7,8},{8,9},{9,10},{10,1... | collective-permute-start | bytes 491528 | tf_op jit(solution)/shard_map/ppermute | solution.py:12
  56.8 8.0 %collective-permute-start.9 = (f32[5,1,32,256]{3,2,1,0:T(8,128)S(1)}, f32[5,1,32,256]{3,2,1,0:T(8,128)S(1)}, u32[]{:S(2)}, u32[]{:S(2)}) collective-permute-start(f32[5,1,32,256]{3,2,1,0:T(8,128)S(1)} %get-tuple-element.23), channel_id=1, source_target_pairs={{0,1},{1,2},{2,3},{3,4},{4,5},{5,6},{6,7},{7,8},{8,9},{9,10},{10,1... | collective-permute-start | bytes 491528 | tf_op jit(solution)/shard_map/ppermute | solution.py:12
  68.7 6.5 %collective-permute-start.11 = (f32[5,1,32,256]{3,2,1,0:T(8,128)S(1)}, f32[5,1,32,256]{3,2,1,0:T(8,128)S(1)}, u32[]{:S(2)}, u32[]{:S(2)}) collective-permute-start(f32[5,1,32,256]{3,2,1,0:T(8,128)S(1)} %get-tuple-element.21), channel_id=1, source_target_pairs={{0,1},{1,2},{2,3},{3,4},{4,5},{5,6},{6,7},{7,8},{8,9},{9,10},{10,1... | collective-permute-start | bytes 491528 | tf_op jit(solution)/shard_map/ppermute | solution.py:12
  79.7 6.5 %collective-permute-start.13 = (f32[5,1,32,256]{3,2,1,0:T(8,128)S(1)}, f32[5,1,32,256]{3,2,1,0:T(8,128)S(1)}, u32[]{:S(2)}, u32[]{:S(2)}) collective-permute-start(f32[5,1,32,256]{3,2,1,0:T(8,128)S(1)} %get-tuple-element.19), channel_id=1, source_target_pairs={{0,1},{1,2},{2,3},{3,4},{4,5},{5,6},{6,7},{7,8},{8,9},{9,10},{10,1... | collective-permute-start | bytes 491528 | tf_op jit(solution)/shard_map/ppermute | solution.py:12
  89.9 4.7 %copy.29 = f32[4,2,32,256]{0,3,2,1:T(8,128)} copy(f32[4,2,32,256]{3,2,1,0:T(8,128)S(1)} %get-tuple-element.15) | data formatting | bytes 524288 | tf_op jit(solution)/shard_map/slice | solution.py:83
  94.6 5.5 %scatter_custom_fusion.1 = f32[4,16384]{0,1:T(8,128)} fusion(s32[64]{0:T(128)S(1)} %get-tuple-element.14, f32[]{:T(128)} %constant.69.clone.1, f32[]{:T(128)} %constant.78.clone.1, f32[64]{0:T(128)S(1)} %copy-done.10, pred[64]{0:T(512)(128)(4,1)S(1)} %get-tuple-element.13, f32[4,16384]{0,1:T(8,128)} %bitcast.125, s32[1024]{0:T(1024)S(1)} %pad_clamp_fusion), kind=kCustom, calls=%fused_computation.27 | custom fusion | flops 768 | bytes 529416 | tf_op jit(solution)/shard_map/scatter-add | solution.py:32
  100.2 5.2 %copy.30 = f32[4,2,32,256]{3,2,1,0:T(8,128)S(1)} copy(f32[4,2,32,256]{0,3,2,1:T(8,128)} %bitcast.126) | data formatting | bytes 524288 | tf_op jit(solution)/shard_map/reshape | solution.py:32
  106.1 6.5 %collective-permute-start.15 = (f32[4,1,32,256]{3,2,1,0:T(8,128)}, f32[4,1,32,256]{3,2,1,0:T(8,128)S(1)}, u32[]{:S(2)}, u32[]{:S(2)}) collective-permute-start(f32[4,1,32,256]{3,2,1,0:T(8,128)} %get-tuple-element.41), channel_id=1, source_target_pairs={{0,1},{1,2},{2,3},{3,4},{4,5},{5,6},{6,7},{7,8},{8,9},{9,10},{10,1... | collective-permute-start | bytes 393224 | tf_op jit(solution)/shard_map/ppermute | solution.py:12
  113.9 4.7 %copy.33 = f32[4,2,32,256]{0,3,2,1:T(8,128)} copy(f32[4,2,32,256]{3,2,1,0:T(8,128)S(1)} %get-tuple-element.16) | data formatting | bytes 524288 | tf_op jit(solution)/shard_map/slice | solution.py:83
  118.6 5.5 %scatter_custom_fusion.2 = f32[4,16384]{0,1:T(8,128)} fusion(s32[64]{0:T(128)S(1)} %get-tuple-element.14, f32[]{:T(128)} %constant.69.clone.1, f32[]{:T(128)} %constant.78.clone.1, f32[64]{0:T(128)S(1)} %copy-done.10, pred[64]{0:T(512)(128)(4,1)S(1)} %get-tuple-element.13, f32[4,16384]{0,1:T(8,128)} %bitcast.127, s32[1024]{0:T(1024)S(1)} %pad_clamp_fusion), kind=kCustom, calls=%fused_computation.25 | custom fusion | flops 768 | bytes 529416 | tf_op jit(solution)/shard_map/scatter-add | solution.py:32
  124.2 5.2 %copy.34 = f32[4,2,32,256]{3,2,1,0:T(8,128)S(1)} copy(f32[4,2,32,256]{0,3,2,1:T(8,128)} %bitcast.128) | data formatting | bytes 524288 | tf_op jit(solution)/shard_map/reshape | solution.py:32
  136.5 4.7 %copy.36 = f32[4,2,32,256]{0,3,2,1:T(8,128)} copy(f32[4,2,32,256]{3,2,1,0:T(8,128)S(1)} %get-tuple-element.17) | data formatting | bytes 524288 | tf_op jit(solution)/shard_map/slice | solution.py:83
  141.2 5.5 %scatter_custom_fusion.3 = f32[4,16384]{0,1:T(8,128)} fusion(s32[64]{0:T(128)S(1)} %get-tuple-element.14, f32[]{:T(128)} %constant.69.clone.1, f32[]{:T(128)} %constant.78.clone.1, f32[64]{0:T(128)S(1)} %copy-done.10, pred[64]{0:T(512)(128)(4,1)S(1)} %get-tuple-element.13, f32[4,16384]{0,1:T(8,128)} %bitcast.129, s32[1024]{0:T(1024)S(1)} %pad_clamp_fusion), kind=kCustom, calls=%fused_computation.23 | custom fusion | flops 768 | bytes 529416 | tf_op jit(solution)/shard_map/scatter-add | solution.py:32
  146.7 5.2 %copy.37 = f32[4,2,32,256]{3,2,1,0:T(8,128)S(1)} copy(f32[4,2,32,256]{0,3,2,1:T(8,128)} %bitcast.130) | data formatting | bytes 524288 | tf_op jit(solution)/shard_map/reshape | solution.py:32
  153.9 5.0 %collective-permute-start.19 = (f32[4,1,32,256]{3,2,1,0:T(8,128)}, f32[4,1,32,256]{3,2,1,0:T(8,128)}, u32[]{:S(2)}, u32[]{:S(2)}) collective-permute-start(f32[4,1,32,256]{3,2,1,0:T(8,128)} %get-tuple-element.37), channel_id=1, source_target_pairs={{0,1},{1,2},{2,3},{3,4},{4,5},{5,6},{6,7},{7,8},{8,9},{9,10},{10,1... | collective-permute-start | bytes 393224 | tf_op jit(solution)/shard_map/ppermute | solution.py:12
  160.2 4.7 %copy.38 = f32[4,2,32,256]{0,3,2,1:T(8,128)} copy(f32[4,2,32,256]{3,2,1,0:T(8,128)S(1)} %slice.584) | data formatting | bytes 524288 | tf_op jit(solution)/shard_map/slice | solution.py:83
  164.9 5.5 %scatter_custom_fusion.4 = f32[4,16384]{0,1:T(8,128)} fusion(s32[64]{0:T(128)S(1)} %get-tuple-element.14, f32[]{:T(128)} %constant.69.clone.1, f32[]{:T(128)} %constant.78.clone.1, f32[64]{0:T(128)S(1)} %copy-done.10, pred[64]{0:T(512)(128)(4,1)S(1)} %get-tuple-element.13, f32[4,16384]{0,1:T(8,128)} %bitcast.131, s32[1024]{0:T(1024)S(1)} %pad_clamp_fusion), kind=kCustom, calls=%fused_computation.21 | custom fusion | flops 768 | bytes 529416 | tf_op jit(solution)/shard_map/scatter-add | solution.py:32
  170.5 5.2 %copy.39 = f32[4,2,32,256]{3,2,1,0:T(8,128)S(1)} copy(f32[4,2,32,256]{0,3,2,1:T(8,128)} %bitcast.132) | data formatting | bytes 524288 | tf_op jit(solution)/shard_map/reshape | solution.py:32
  183.2 4.7 %copy.40 = f32[4,2,32,256]{0,3,2,1:T(8,128)} copy(f32[4,2,32,256]{3,2,1,0:T(8,128)S(1)} %slice.587) | data formatting | bytes 524288 | tf_op jit(solution)/shard_map/slice | solution.py:83
  188.0 5.5 %scatter_custom_fusion.5 = f32[4,16384]{0,1:T(8,128)} fusion(s32[64]{0:T(128)S(1)} %get-tuple-element.14, f32[]{:T(128)} %constant.69.clone.1, f32[]{:T(128)} %constant.78.clone.1, f32[64]{0:T(128)S(1)} %copy-done.10, pred[64]{0:T(512)(128)(4,1)S(1)} %get-tuple-element.13, f32[4,16384]{0,1:T(8,128)} %bitcast.133, s32[1024]{0:T(1024)S(1)} %pad_clamp_fusion), kind=kCustom, calls=%fused_computation.19 | custom fusion | flops 768 | bytes 529416 | tf_op jit(solution)/shard_map/scatter-add | solution.py:32
  193.5 5.2 %copy.41 = f32[4,2,32,256]{3,2,1,0:T(8,128)S(1)} copy(f32[4,2,32,256]{0,3,2,1:T(8,128)} %bitcast.134) | data formatting | bytes 524288 | tf_op jit(solution)/shard_map/reshape | solution.py:32
  205.6 4.7 %copy.42 = f32[4,2,32,256]{0,3,2,1:T(8,128)} copy(f32[4,2,32,256]{3,2,1,0:T(8,128)S(1)} %slice.590) | data formatting | bytes 524288 | tf_op jit(solution)/shard_map/slice | solution.py:83
  210.3 5.5 %scatter_custom_fusion.6 = f32[4,16384]{0,1:T(8,128)} fusion(s32[64]{0:T(128)S(1)} %get-tuple-element.14, f32[]{:T(128)} %constant.69.clone.1, f32[]{:T(128)} %constant.78.clone.1, f32[64]{0:T(128)S(1)} %copy-done.10, pred[64]{0:T(512)(128)(4,1)S(1)} %get-tuple-element.13, f32[4,16384]{0,1:T(8,128)} %bitcast.135, s32[1024]{0:T(1024)S(1)} %pad_clamp_fusion), kind=kCustom, calls=%fused_computation.17 | custom fusion | flops 768 | bytes 529416 | tf_op jit(solution)/shard_map/scatter-add | solution.py:32
  215.9 5.2 %copy.43 = f32[4,2,32,256]{3,2,1,0:T(8,128)S(1)} copy(f32[4,2,32,256]{0,3,2,1:T(8,128)} %bitcast.136) | data formatting | bytes 524288 | tf_op jit(solution)/shard_map/reshape | solution.py:32
  227.5 4.7 %copy.44 = f32[4,2,32,256]{0,3,2,1:T(8,128)} copy(f32[4,2,32,256]{3,2,1,0:T(8,128)S(1)} %slice.593) | data formatting | bytes 524288 | tf_op jit(solution)/shard_map/slice | solution.py:83
  232.3 5.5 %scatter_custom_fusion.7 = f32[4,16384]{0,1:T(8,128)} fusion(s32[64]{0:T(128)S(1)} %get-tuple-element.14, f32[]{:T(128)} %constant.69.clone.1, f32[]{:T(128)} %constant.78.clone.1, f32[64]{0:T(128)S(1)} %copy-done.10, pred[64]{0:T(512)(128)(4,1)S(1)} %get-tuple-element.13, f32[4,16384]{0,1:T(8,128)} %bitcast.123, s32[1024]{0:T(1024)S(1)} %pad_clamp_fusion), kind=kCustom, calls=%fused_computation.15 | custom fusion | flops 768 | bytes 529416 | tf_op jit(solution)/shard_map/scatter-add | solution.py:32
  237.8 5.3 %copy.45 = f32[4,2,32,256]{3,2,1,0:T(8,128)S(1)} copy(f32[4,2,32,256]{0,3,2,1:T(8,128)} %bitcast.124) | data formatting | bytes 524288 | tf_op jit(solution)/shard_map/reshape | solution.py:32
  246.0 45.0 %all-gather.3.cloned.1.call-done = f32[4,4,16384]{2,1,0:T(4,128)} async-done(((f32[1,4,16384]{2,1,0:T(4,128)}), f32[4,4,16384]{2,1,0:T(4,128)}) %all-gather.3.cloned.1.call-update) | async-done | bytes 1048592 | tf_op jit(solution)/shard_map/all_gather | solution.py:97
  294.1 129.5 %psum.7 = f32[16,16]{0,1:T(8,128)S(1)} all-reduce(f32[16,16]{0,1:T(8,128)S(1)} %fusion.185), channel_id=1, replica_groups=mesh['probe'=4,'space'=64] {'space'}, use_global_device_ids=true, to_apply=%region_8.10 | all-reduce | flops 256 | bytes 2048 | tf_op jit(solution)/shard_map/psum | solution.py:98
  (150 shorter events, 84.1 us)
Async XLA Ops:
  7.2 39.8 %copy-start = (f32[2,32,256]{2,1,0:T(8,128)S(1)}, f32[2,32,256]{2,1,0:T(8,128)}, u32[]{:S(2)}) copy-start(f32[2,32,256]{2,1,0:T(8,128)} %param.10) | copy-start | bytes 196612
  7.2 39.8 %copy-start.1 = (f32[4,2,32,256]{3,2,1,0:T(8,128)S(1)}, f32[4,2,32,256]{3,2,1,0:T(8,128)}, u32[]{:S(2)}) copy-start(f32[4,2,32,256]{3,2,1,0:T(8,128)} %param.11) | copy-start | bytes 786436
  7.2 283.8 %all-gather.3.cloned.1.call-start = ((), (), s32[]{:S(2)}) async-start(), calls=%async_computation | async-start | bytes 1310720 | tf_op jit(solution)/shard_map/all_gather | solution.py:97
  15.7 3.1 collective-permute-start.1
  17.4 5.0 %collective-permute-start = (f32[5,1,32,256]{3,2,1,0:T(8,128)S(1)}, f32[5,1,32,256]{3,2,1,0:T(8,128)S(1)}, u32[]{:S(2)}, u32[]{:S(2)}) collective-permute-start(f32[5,1,32,256]{3,2,1,0:T(8,128)S(1)} %get-tuple-element.50), channel_id=1, source_target_pairs={{1,0},{2,1},{3,2},{4,3},{5,4},{6,5},{7,6},{8,7},{9,8},{10,9},{11,1... | collective-permute-start | bytes 491528 | tf_op jit(solution)/shard_map/ppermute | solution.py:15
  25.6 7.1 %collective-permute-start.3 = (f32[5,1,32,256]{3,2,1,0:T(8,128)S(1)}, f32[5,1,32,256]{3,2,1,0:T(8,128)S(1)}, u32[]{:S(2)}, u32[]{:S(2)}) collective-permute-start(f32[5,1,32,256]{3,2,1,0:T(8,128)S(1)} %get-tuple-element.29), channel_id=1, source_target_pairs={{0,1},{1,2},{2,3},{3,4},{4,5},{5,6},{6,7},{7,8},{8,9},{9,10},{10,1... | collective-permute-start | bytes 491528 | tf_op jit(solution)/shard_map/ppermute | solution.py:12
  31.4 3.3 collective-permute-start.2
  37.9 6.9 %collective-permute-start.5 = (f32[5,1,32,256]{3,2,1,0:T(8,128)S(1)}, f32[5,1,32,256]{3,2,1,0:T(8,128)S(1)}, u32[]{:S(2)}, u32[]{:S(2)}) collective-permute-start(f32[5,1,32,256]{3,2,1,0:T(8,128)S(1)} %get-tuple-element.27), channel_id=1, source_target_pairs={{0,1},{1,2},{2,3},{3,4},{4,5},{5,6},{6,7},{7,8},{8,9},{9,10},{10,1... | collective-permute-start | bytes 491528 | tf_op jit(solution)/shard_map/ppermute | solution.py:12
  43.4 3.3 collective-permute-start.4
  44.8 42.8 %copy-start.11 = (s32[64]{0:T(128)S(1)}, s32[64]{0:T(128)}, u32[]{:S(2)}) copy-start(s32[64]{0:T(128)} %param.16) | copy-start | bytes 772
  47.4 6.9 %collective-permute-start.7 = (f32[5,1,32,256]{3,2,1,0:T(8,128)S(1)}, f32[5,1,32,256]{3,2,1,0:T(8,128)S(1)}, u32[]{:S(2)}, u32[]{:S(2)}) collective-permute-start(f32[5,1,32,256]{3,2,1,0:T(8,128)S(1)} %get-tuple-element.25), channel_id=1, source_target_pairs={{0,1},{1,2},{2,3},{3,4},{4,5},{5,6},{6,7},{7,8},{8,9},{9,10},{10,1... | collective-permute-start | bytes 491528 | tf_op jit(solution)/shard_map/ppermute | solution.py:12
  52.9 3.3 collective-permute-start.6
  56.8 9.3 %collective-permute-start.9 = (f32[5,1,32,256]{3,2,1,0:T(8,128)S(1)}, f32[5,1,32,256]{3,2,1,0:T(8,128)S(1)}, u32[]{:S(2)}, u32[]{:S(2)}) collective-permute-start(f32[5,1,32,256]{3,2,1,0:T(8,128)S(1)} %get-tuple-element.23), channel_id=1, source_target_pairs={{0,1},{1,2},{2,3},{3,4},{4,5},{5,6},{6,7},{7,8},{8,9},{9,10},{10,1... | collective-permute-start | bytes 491528 | tf_op jit(solution)/shard_map/ppermute | solution.py:12
  64.8 3.3 collective-permute-start.8
  68.7 7.8 %collective-permute-start.11 = (f32[5,1,32,256]{3,2,1,0:T(8,128)S(1)}, f32[5,1,32,256]{3,2,1,0:T(8,128)S(1)}, u32[]{:S(2)}, u32[]{:S(2)}) collective-permute-start(f32[5,1,32,256]{3,2,1,0:T(8,128)S(1)} %get-tuple-element.21), channel_id=1, source_target_pairs={{0,1},{1,2},{2,3},{3,4},{4,5},{5,6},{6,7},{7,8},{8,9},{9,10},{10,1... | collective-permute-start | bytes 491528 | tf_op jit(solution)/shard_map/ppermute | solution.py:12
  75.2 3.3 collective-permute-start.10
  76.5 18.1 %copy-start.10 = (f32[64]{0:T(128)S(1)}, f32[64]{0:T(128)}, u32[]{:S(2)}) copy-start(f32[64]{0:T(128)} %param.17) | copy-start | bytes 772
  79.7 7.9 %collective-permute-start.13 = (f32[5,1,32,256]{3,2,1,0:T(8,128)S(1)}, f32[5,1,32,256]{3,2,1,0:T(8,128)S(1)}, u32[]{:S(2)}, u32[]{:S(2)}) collective-permute-start(f32[5,1,32,256]{3,2,1,0:T(8,128)S(1)} %get-tuple-element.19), channel_id=1, source_target_pairs={{0,1},{1,2},{2,3},{3,4},{4,5},{5,6},{6,7},{7,8},{8,9},{9,10},{10,1... | collective-permute-start | bytes 491528 | tf_op jit(solution)/shard_map/ppermute | solution.py:12
  86.2 3.3 collective-permute-start.12
  106.1 23.3 %collective-permute-start.15 = (f32[4,1,32,256]{3,2,1,0:T(8,128)}, f32[4,1,32,256]{3,2,1,0:T(8,128)S(1)}, u32[]{:S(2)}, u32[]{:S(2)}) collective-permute-start(f32[4,1,32,256]{3,2,1,0:T(8,128)} %get-tuple-element.41), channel_id=1, source_target_pairs={{0,1},{1,2},{2,3},{3,4},{4,5},{5,6},{6,7},{7,8},{8,9},{9,10},{10,1... | collective-permute-start | bytes 393224 | tf_op jit(solution)/shard_map/ppermute | solution.py:12
  112.6 17.5 %collective-permute-start.14 = (f32[4,1,32,256]{3,2,1,0:T(8,128)S(1)}, f32[4,1,32,256]{3,2,1,0:T(8,128)}, u32[]{:S(2)}, u32[]{:S(2)}) collective-permute-start(f32[4,1,32,256]{3,2,1,0:T(8,128)S(1)} %get-tuple-element.40), channel_id=1, source_target_pairs={{1,0},{2,1},{3,2},{4,3},{5,4},{6,5},{7,6},{8,7},{9,8},{10,9},{11,1... | collective-permute-start | bytes 393224 | tf_op jit(solution)/shard_map/ppermute | solution.py:15
  131.3 20.7 %collective-permute-start.17 = (f32[4,1,32,256]{3,2,1,0:T(8,128)S(1)}, f32[4,1,32,256]{3,2,1,0:T(8,128)}, u32[]{:S(2)}, u32[]{:S(2)}) collective-permute-start(f32[4,1,32,256]{3,2,1,0:T(8,128)S(1)} %get-tuple-element.39), channel_id=1, source_target_pairs={{0,1},{1,2},{2,3},{3,4},{4,5},{5,6},{6,7},{7,8},{8,9},{9,10},{10,1... | collective-permute-start | bytes 393224 | tf_op jit(solution)/shard_map/ppermute | solution.py:12
  135.0 17.0 %collective-permute-start.16 = (f32[4,1,32,256]{3,2,1,0:T(8,128)S(1)}, f32[4,1,32,256]{3,2,1,0:T(8,128)}, u32[]{:S(2)}, u32[]{:S(2)}) collective-permute-start(f32[4,1,32,256]{3,2,1,0:T(8,128)S(1)} %get-tuple-element.38), channel_id=1, source_target_pairs={{1,0},{2,1},{3,2},{4,3},{5,4},{6,5},{7,6},{8,7},{9,8},{10,9},{11,1... | collective-permute-start | bytes 393224 | tf_op jit(solution)/shard_map/ppermute | solution.py:15
  153.9 21.8 %collective-permute-start.19 = (f32[4,1,32,256]{3,2,1,0:T(8,128)}, f32[4,1,32,256]{3,2,1,0:T(8,128)}, u32[]{:S(2)}, u32[]{:S(2)}) collective-permute-start(f32[4,1,32,256]{3,2,1,0:T(8,128)} %get-tuple-element.37), channel_id=1, source_target_pairs={{0,1},{1,2},{2,3},{3,4},{4,5},{5,6},{6,7},{7,8},{8,9},{9,10},{10,1... | collective-permute-start | bytes 393224 | tf_op jit(solution)/shard_map/ppermute | solution.py:12
  158.9 16.8 %collective-permute-start.18 = (f32[4,1,32,256]{3,2,1,0:T(8,128)}, f32[4,1,32,256]{3,2,1,0:T(8,128)}, u32[]{:S(2)}, u32[]{:S(2)}) collective-permute-start(f32[4,1,32,256]{3,2,1,0:T(8,128)} %get-tuple-element.36), channel_id=1, source_target_pairs={{1,0},{2,1},{3,2},{4,3},{5,4},{6,5},{7,6},{8,7},{9,8},{10,9},{11,1... | collective-permute-start | bytes 393224 | tf_op jit(solution)/shard_map/ppermute | solution.py:15
  177.7 21.1 %collective-permute-start.21 = (f32[4,1,32,256]{3,2,1,0:T(8,128)}, f32[4,1,32,256]{3,2,1,0:T(8,128)}, u32[]{:S(2)}, u32[]{:S(2)}) collective-permute-start(f32[4,1,32,256]{3,2,1,0:T(8,128)} %get-tuple-element.35), channel_id=1, source_target_pairs={{0,1},{1,2},{2,3},{3,4},{4,5},{5,6},{6,7},{7,8},{8,9},{9,10},{10,1... | collective-permute-start | bytes 393224 | tf_op jit(solution)/shard_map/ppermute | solution.py:12
  181.9 16.8 %collective-permute-start.20 = (f32[4,1,32,256]{3,2,1,0:T(8,128)}, f32[4,1,32,256]{3,2,1,0:T(8,128)}, u32[]{:S(2)}, u32[]{:S(2)}) collective-permute-start(f32[4,1,32,256]{3,2,1,0:T(8,128)} %get-tuple-element.34), channel_id=1, source_target_pairs={{1,0},{2,1},{3,2},{4,3},{5,4},{6,5},{7,6},{8,7},{9,8},{10,9},{11,1... | collective-permute-start | bytes 393224 | tf_op jit(solution)/shard_map/ppermute | solution.py:15
  200.0 21.1 %collective-permute-start.23 = (f32[4,1,32,256]{3,2,1,0:T(8,128)S(1)}, f32[4,1,32,256]{3,2,1,0:T(8,128)}, u32[]{:S(2)}, u32[]{:S(2)}) collective-permute-start(f32[4,1,32,256]{3,2,1,0:T(8,128)S(1)} %get-tuple-element.33), channel_id=1, source_target_pairs={{0,1},{1,2},{2,3},{3,4},{4,5},{5,6},{6,7},{7,8},{8,9},{9,10},{10,1... | collective-permute-start | bytes 393224 | tf_op jit(solution)/shard_map/ppermute | solution.py:12
  204.3 16.8 %collective-permute-start.22 = (f32[4,1,32,256]{3,2,1,0:T(8,128)S(1)}, f32[4,1,32,256]{3,2,1,0:T(8,128)}, u32[]{:S(2)}, u32[]{:S(2)}) collective-permute-start(f32[4,1,32,256]{3,2,1,0:T(8,128)S(1)} %get-tuple-element.32), channel_id=1, source_target_pairs={{1,0},{2,1},{3,2},{4,3},{5,4},{6,5},{7,6},{8,7},{9,8},{10,9},{11,1... | collective-permute-start | bytes 393224 | tf_op jit(solution)/shard_map/ppermute | solution.py:15
  222.3 20.7 %collective-permute-start.25 = (f32[4,1,32,256]{3,2,1,0:T(8,128)S(1)}, f32[4,1,32,256]{3,2,1,0:T(8,128)S(1)}, u32[]{:S(2)}, u32[]{:S(2)}) collective-permute-start(f32[4,1,32,256]{3,2,1,0:T(8,128)S(1)} %get-tuple-element.31), channel_id=1, source_target_pairs={{0,1},{1,2},{2,3},{3,4},{4,5},{5,6},{6,7},{7,8},{8,9},{9,10},{10,1... | collective-permute-start | bytes 393224 | tf_op jit(solution)/shard_map/ppermute | solution.py:12
  226.0 17.1 %collective-permute-start.24 = (f32[4,1,32,256]{3,2,1,0:T(8,128)S(1)}, f32[4,1,32,256]{3,2,1,0:T(8,128)}, u32[]{:S(2)}, u32[]{:S(2)}) collective-permute-start(f32[4,1,32,256]{3,2,1,0:T(8,128)S(1)} %get-tuple-element.30), channel_id=1, source_target_pairs={{1,0},{2,1},{3,2},{4,3},{5,4},{6,5},{7,6},{8,7},{9,8},{10,9},{11,1... | collective-permute-start | bytes 393224 | tf_op jit(solution)/shard_map/ppermute | solution.py:15
  245.1 184.5 %copy-start.2 = (f32[4,2,32,256]{3,2,1,0:T(8,128)}, f32[4,2,32,256]{3,2,1,0:T(8,128)S(1)}, u32[]{:S(2)}) copy-start(f32[4,2,32,256]{3,2,1,0:T(8,128)S(1)} %fusion.103) | copy-start | bytes 786436
  (7 other events, 30.2 us)
Sparse Core Ops, SparseCore 0:
  246.1 44.8 all-gather.2
where the time goes:
time: 438 us; the launch traced here: 436 us
  blocking collectives  129 us (29%)
  starting transfers between devices  84.1 us (19%)
  local copies, waits for them, and re-layouts  79.3 us (18%)
  other arithmetic  65.7 us (15%)
  waiting for transfers between devices  60.3 us (14%)
  between operations  15 us (3%)
    psum x1, blocking collectives, shards(): gram = lax.psum(inner_rows(rows), 'space') / total_cells  129 us
    ppermute x13, starting transfers between devices, extended(): lax.ppermute(lax.slice_in_dim(block, block.shape[dim] - width, None, axis...  66.9 us
    all_gather x1, waiting for transfers between devices, shards(): rows = lax.all_gather(flat, 'probe', axis=0, tiled=True)  45 us
    scatter-add x7, other arithmetic, inject(): return flat.at[:, local_cells].add(values).reshape(field_shape)  38.7 us
    reshape x7, local copies, waits for them, and re-layouts, inject(): return flat.at[:, local_cells].add(values).reshape(field_shape)  36.7 us
    slice x11, local copies, waits for them, and re-layouts, shards(): state_next[1:].reshape(groups, cells)  33.2 us
    ppermute x13, starting transfers between devices, extended(): lax.ppermute(lax.slice_in_dim(block, 0, width, axis=dim), axis, backward)  17.1 us
    ppermute x13, waiting for transfers between devices, extended(): lax.ppermute(lax.slice_in_dim(block, 0, width, axis=dim), axis, backward)  15.3 us
  transfers between devices with their start and end apart: 27, of which 8 were waited for; matrix products, arithmetic and copies ran while one was open for 21% of the time, Pallas kernels for 0%

commit v1 on v0

--- a/solution.py
+++ b/solution.py
@@ -95,7 +95,7 @@
     flat = hessian.reshape(groups, cells)
     total_cells = cells * lax.axis_size("space")
     rows = lax.all_gather(flat, "probe", axis=0, tiled=True)
-    gram = lax.psum(inner_rows(rows), "space") / total_cells
+    gram = jnp.sum(lax.all_gather(inner_rows(rows), "space"), axis=0) / total_cells
     lower = jnp.linalg.cholesky(gram)
     solved = lax.linalg.triangular_solve(lower, rows, left_side=True, lower=True)
     mine = lax.dynamic_slice_in_dim(solved, lax.axis_index("probe") * groups, groups, 0)

time: 438 us -> 360 us (0.82)
  blocking collectives: 129 us -> 51.3 us
    psum x1 -> x0, blocking collectives: 129 us -> none  [shards(): gram = lax.psum(inner_rows(rows), 'space') / total_cells]
    all_gather x0 -> x1, blocking collectives: none -> 51.3 us  [shards(): lax.all_gather(inner_rows(rows), 'space')]
  transfers between devices with their start and end apart: 27 -> 27, of which waited for: 8 -> 8; matrix products, arithmetic and copies ran while one was open for 21% -> 26% of each run, Pallas kernels for 0% -> 0%
where the time goes in v1:
time: 360 us; the launch traced here: 356 us
  starting transfers between devices  84.1 us (23%)
  local copies, waits for them, and re-layouts  79.8 us (22%)
  other arithmetic  63.1 us (18%)
  waiting for transfers between devices  60.4 us (17%)
  blocking collectives  51.3 us (14%)
  between operations  15.1 us (4%)
    ppermute x13, starting transfers between devices, extended(): lax.ppermute(lax.slice_in_dim(block, block.shape[dim] - width, None, axis...  66.9 us
    all_gather x1, blocking collectives, shards(): lax.all_gather(inner_rows(rows), 'space')  51.3 us
    all_gather x1, waiting for transfers between devices, shards(): rows = lax.all_gather(flat, 'probe', axis=0, tiled=True)  45.1 us
    scatter-add x7, other arithmetic, inject(): return flat.at[:, local_cells].add(values).reshape(field_shape)  39 us
    reshape x7, local copies, waits for them, and re-layouts, inject(): return flat.at[:, local_cells].add(values).reshape(field_shape)  36.7 us
    slice x11, local copies, waits for them, and re-layouts, shards(): state_next[1:].reshape(groups, cells)  33.2 us
    ppermute x13, starting transfers between devices, extended(): lax.ppermute(lax.slice_in_dim(block, 0, width, axis=dim), axis, backward)  17.2 us
    ppermute x13, waiting for transfers between devices, extended(): lax.ppermute(lax.slice_in_dim(block, 0, width, axis=dim), axis, backward)  15.3 us
  transfers between devices with their start and end apart: 27, of which 8 were waited for; matrix products, arithmetic and copies ran while one was open for 26% of the time, Pallas kernels for 0%

profile of v1, /device:TPU:4, one launch (start us, length us, event | category | flops | bytes accessed | tf_op | source)
XLA Modules:
  0.0 356.3 jit_solution(1140678241477410485)
XLA Ops:
  10.6 5.0 %broadcast_multiply_fusion.13 = (f32[16384]{0:T(1024)S(1)}, f32[16384]{0:T(1024)S(1)}, f32[16384]{0:T(1024)S(1)}, f32[16384]{0:T(1024)S(1)}, f32[16384]{0:T(1024...) fusion(f32[16384]{0:T(1024)S(1)} %scatter_custom_fusion, f32[]{:T(128)} %bitcast.14, f32[]{:T(128)} %bitcast.11, ...), kind=kLoop, calls=%fused_computation.264 | loop fusion | flops 131072 | bytes 589856 | tf_op jit(solution)/shard_map/mul | solution.py:79
  25.6 5.8 %collective-permute-start.3 = (f32[5,1,32,256]{3,2,1,0:T(8,128)S(1)}, f32[5,1,32,256]{3,2,1,0:T(8,128)S(1)}, u32[]{:S(2)}, u32[]{:S(2)}) collective-permute-start(f32[5,1,32,256]{3,2,1,0:T(8,128)S(1)} %get-tuple-element.29), channel_id=1, source_target_pairs={{0,1},{1,2},{2,3},{3,4},{4,5},{5,6},{6,7},{7,8},{8,9},{9,10},{10,1... | collective-permute-start | bytes 491528 | tf_op jit(solution)/shard_map/ppermute | solution.py:12
  38.5 5.6 %collective-permute-start.5 = (f32[5,1,32,256]{3,2,1,0:T(8,128)S(1)}, f32[5,1,32,256]{3,2,1,0:T(8,128)S(1)}, u32[]{:S(2)}, u32[]{:S(2)}) collective-permute-start(f32[5,1,32,256]{3,2,1,0:T(8,128)S(1)} %get-tuple-element.27), channel_id=1, source_target_pairs={{0,1},{1,2},{2,3},{3,4},{4,5},{5,6},{6,7},{7,8},{8,9},{9,10},{10,1... | collective-permute-start | bytes 491528 | tf_op jit(solution)/shard_map/ppermute | solution.py:12
  48.6 5.6 %collective-permute-start.7 = (f32[5,1,32,256]{3,2,1,0:T(8,128)S(1)}, f32[5,1,32,256]{3,2,1,0:T(8,128)S(1)}, u32[]{:S(2)}, u32[]{:S(2)}) collective-permute-start(f32[5,1,32,256]{3,2,1,0:T(8,128)S(1)} %get-tuple-element.25), channel_id=1, source_target_pairs={{0,1},{1,2},{2,3},{3,4},{4,5},{5,6},{6,7},{7,8},{8,9},{9,10},{10,1... | collective-permute-start | bytes 491528 | tf_op jit(solution)/shard_map/ppermute | solution.py:12
  58.6 8.0 %collective-permute-start.9 = (f32[5,1,32,256]{3,2,1,0:T(8,128)S(1)}, f32[5,1,32,256]{3,2,1,0:T(8,128)S(1)}, u32[]{:S(2)}, u32[]{:S(2)}) collective-permute-start(f32[5,1,32,256]{3,2,1,0:T(8,128)S(1)} %get-tuple-element.23), channel_id=1, source_target_pairs={{0,1},{1,2},{2,3},{3,4},{4,5},{5,6},{6,7},{7,8},{8,9},{9,10},{10,1... | collective-permute-start | bytes 491528 | tf_op jit(solution)/shard_map/ppermute | solution.py:12
  71.2 6.5 %collective-permute-start.11 = (f32[5,1,32,256]{3,2,1,0:T(8,128)S(1)}, f32[5,1,32,256]{3,2,1,0:T(8,128)S(1)}, u32[]{:S(2)}, u32[]{:S(2)}) collective-permute-start(f32[5,1,32,256]{3,2,1,0:T(8,128)S(1)} %get-tuple-element.21), channel_id=1, source_target_pairs={{0,1},{1,2},{2,3},{3,4},{4,5},{5,6},{6,7},{7,8},{8,9},{9,10},{10,1... | collective-permute-start | bytes 491528 | tf_op jit(solution)/shard_map/ppermute | solution.py:12
  82.2 6.5 %collective-permute-start.13 = (f32[5,1,32,256]{3,2,1,0:T(8,128)S(1)}, f32[5,1,32,256]{3,2,1,0:T(8,128)S(1)}, u32[]{:S(2)}, u32[]{:S(2)}) collective-permute-start(f32[5,1,32,256]{3,2,1,0:T(8,128)S(1)} %get-tuple-element.19), channel_id=1, source_target_pairs={{0,1},{1,2},{2,3},{3,4},{4,5},{5,6},{6,7},{7,8},{8,9},{9,10},{10,1... | collective-permute-start | bytes 491528 | tf_op jit(solution)/shard_map/ppermute | solution.py:12
  92.4 4.7 %copy.28 = f32[4,2,32,256]{0,3,2,1:T(8,128)} copy(f32[4,2,32,256]{3,2,1,0:T(8,128)S(1)} %get-tuple-element.15) | data formatting | bytes 524288 | tf_op jit(solution)/shard_map/slice | solution.py:83
  97.1 5.6 %scatter_custom_fusion.1 = f32[4,16384]{0,1:T(8,128)} fusion(s32[64]{0:T(128)S(1)} %get-tuple-element.14, f32[]{:T(128)} %constant.71.clone.1, f32[]{:T(128)} %constant.79.clone.1, f32[64]{0:T(128)S(1)} %copy-done.18, pred[64]{0:T(512)(128)(4,1)S(1)} %get-tuple-element.13, f32[4,16384]{0,1:T(8,128)} %bitcast.126, s32[1024]{0:T(1024)S(1)} %pad_clamp_fusion), kind=kCustom, calls=%fused_computation.27 | custom fusion | flops 768 | bytes 529416 | tf_op jit(solution)/shard_map/scatter-add | solution.py:32
  102.7 5.2 %copy.29 = f32[4,2,32,256]{3,2,1,0:T(8,128)S(1)} copy(f32[4,2,32,256]{0,3,2,1:T(8,128)} %bitcast.127) | data formatting | bytes 524288 | tf_op jit(solution)/shard_map/reshape | solution.py:32
  108.0 6.5 %collective-permute-start.15 = (f32[4,1,32,256]{3,2,1,0:T(8,128)S(1)}, f32[4,1,32,256]{3,2,1,0:T(8,128)S(1)}, u32[]{:S(2)}, u32[]{:S(2)}) collective-permute-start(f32[4,1,32,256]{3,2,1,0:T(8,128)S(1)} %get-tuple-element.41), channel_id=1, source_target_pairs={{0,1},{1,2},{2,3},{3,4},{4,5},{5,6},{6,7},{7,8},{8,9},{9,10},{10,1... | collective-permute-start | bytes 393224 | tf_op jit(solution)/shard_map/ppermute | solution.py:12
  115.8 4.7 %copy.32 = f32[4,2,32,256]{0,3,2,1:T(8,128)} copy(f32[4,2,32,256]{3,2,1,0:T(8,128)S(1)} %get-tuple-element.16) | data formatting | bytes 524288 | tf_op jit(solution)/shard_map/slice | solution.py:83
  120.5 5.6 %scatter_custom_fusion.2 = f32[4,16384]{0,1:T(8,128)} fusion(s32[64]{0:T(128)S(1)} %get-tuple-element.14, f32[]{:T(128)} %constant.71.clone.1, f32[]{:T(128)} %constant.79.clone.1, f32[64]{0:T(128)S(1)} %copy-done.18, pred[64]{0:T(512)(128)(4,1)S(1)} %get-tuple-element.13, f32[4,16384]{0,1:T(8,128)} %bitcast.128, s32[1024]{0:T(1024)S(1)} %pad_clamp_fusion), kind=kCustom, calls=%fused_computation.25 | custom fusion | flops 768 | bytes 529416 | tf_op jit(solution)/shard_map/scatter-add | solution.py:32
  126.1 5.2 %copy.33 = f32[4,2,32,256]{3,2,1,0:T(8,128)S(1)} copy(f32[4,2,32,256]{0,3,2,1:T(8,128)} %bitcast.129) | data formatting | bytes 524288 | tf_op jit(solution)/shard_map/reshape | solution.py:32
  136.1 4.7 %copy.35 = f32[4,2,32,256]{0,3,2,1:T(8,128)} copy(f32[4,2,32,256]{3,2,1,0:T(8,128)S(1)} %get-tuple-element.17) | data formatting | bytes 524288 | tf_op jit(solution)/shard_map/slice | solution.py:83
  140.9 5.6 %scatter_custom_fusion.3 = f32[4,16384]{0,1:T(8,128)} fusion(s32[64]{0:T(128)S(1)} %get-tuple-element.14, f32[]{:T(128)} %constant.71.clone.1, f32[]{:T(128)} %constant.79.clone.1, f32[64]{0:T(128)S(1)} %copy-done.18, pred[64]{0:T(512)(128)(4,1)S(1)} %get-tuple-element.13, f32[4,16384]{0,1:T(8,128)} %bitcast.130, s32[1024]{0:T(1024)S(1)} %pad_clamp_fusion), kind=kCustom, calls=%fused_computation.23 | custom fusion | flops 768 | bytes 529416 | tf_op jit(solution)/shard_map/scatter-add | solution.py:32
  146.4 5.2 %copy.36 = f32[4,2,32,256]{3,2,1,0:T(8,128)S(1)} copy(f32[4,2,32,256]{0,3,2,1:T(8,128)} %bitcast.131) | data formatting | bytes 524288 | tf_op jit(solution)/shard_map/reshape | solution.py:32
  151.9 5.6 %collective-permute-start.19 = (f32[4,1,32,256]{3,2,1,0:T(8,128)S(1)}, f32[4,1,32,256]{3,2,1,0:T(8,128)}, u32[]{:S(2)}, u32[]{:S(2)}) collective-permute-start(f32[4,1,32,256]{3,2,1,0:T(8,128)S(1)} %get-tuple-element.37), channel_id=1, source_target_pairs={{0,1},{1,2},{2,3},{3,4},{4,5},{5,6},{6,7},{7,8},{8,9},{9,10},{10,1... | collective-permute-start | bytes 393224 | tf_op jit(solution)/shard_map/ppermute | solution.py:12
  158.9 4.7 %copy.37 = f32[4,2,32,256]{0,3,2,1:T(8,128)} copy(f32[4,2,32,256]{3,2,1,0:T(8,128)S(1)} %slice.584) | data formatting | bytes 524288 | tf_op jit(solution)/shard_map/slice | solution.py:83
  163.6 5.6 %scatter_custom_fusion.4 = f32[4,16384]{0,1:T(8,128)} fusion(s32[64]{0:T(128)S(1)} %get-tuple-element.14, f32[]{:T(128)} %constant.71.clone.1, f32[]{:T(128)} %constant.79.clone.1, f32[64]{0:T(128)S(1)} %copy-done.18, pred[64]{0:T(512)(128)(4,1)S(1)} %get-tuple-element.13, f32[4,16384]{0,1:T(8,128)} %bitcast.132, s32[1024]{0:T(1024)S(1)} %pad_clamp_fusion), kind=kCustom, calls=%fused_computation.21 | custom fusion | flops 768 | bytes 529416 | tf_op jit(solution)/shard_map/scatter-add | solution.py:32
  169.2 5.2 %copy.38 = f32[4,2,32,256]{3,2,1,0:T(8,128)S(1)} copy(f32[4,2,32,256]{0,3,2,1:T(8,128)} %bitcast.133) | data formatting | bytes 524288 | tf_op jit(solution)/shard_map/reshape | solution.py:32
  181.3 4.7 %copy.39 = f32[4,2,32,256]{0,3,2,1:T(8,128)} copy(f32[4,2,32,256]{3,2,1,0:T(8,128)S(1)} %slice.587) | data formatting | bytes 524288 | tf_op jit(solution)/shard_map/slice | solution.py:83
  186.0 5.6 %scatter_custom_fusion.5 = f32[4,16384]{0,1:T(8,128)} fusion(s32[64]{0:T(128)S(1)} %get-tuple-element.14, f32[]{:T(128)} %constant.71.clone.1, f32[]{:T(128)} %constant.79.clone.1, f32[64]{0:T(128)S(1)} %copy-done.18, pred[64]{0:T(512)(128)(4,1)S(1)} %get-tuple-element.13, f32[4,16384]{0,1:T(8,128)} %bitcast.134, s32[1024]{0:T(1024)S(1)} %pad_clamp_fusion), kind=kCustom, calls=%fused_computation.19 | custom fusion | flops 768 | bytes 529416 | tf_op jit(solution)/shard_map/scatter-add | solution.py:32
  191.6 5.2 %copy.40 = f32[4,2,32,256]{3,2,1,0:T(8,128)S(1)} copy(f32[4,2,32,256]{0,3,2,1:T(8,128)} %bitcast.135) | data formatting | bytes 524288 | tf_op jit(solution)/shard_map/reshape | solution.py:32
  203.0 4.7 %copy.41 = f32[4,2,32,256]{0,3,2,1:T(8,128)} copy(f32[4,2,32,256]{3,2,1,0:T(8,128)S(1)} %slice.590) | data formatting | bytes 524288 | tf_op jit(solution)/shard_map/slice | solution.py:83
  207.8 5.6 %scatter_custom_fusion.6 = f32[4,16384]{0,1:T(8,128)} fusion(s32[64]{0:T(128)S(1)} %get-tuple-element.14, f32[]{:T(128)} %constant.71.clone.1, f32[]{:T(128)} %constant.79.clone.1, f32[64]{0:T(128)S(1)} %copy-done.18, pred[64]{0:T(512)(128)(4,1)S(1)} %get-tuple-element.13, f32[4,16384]{0,1:T(8,128)} %bitcast.136, s32[1024]{0:T(1024)S(1)} %pad_clamp_fusion), kind=kCustom, calls=%fused_computation.17 | custom fusion | flops 768 | bytes 529416 | tf_op jit(solution)/shard_map/scatter-add | solution.py:32
  213.3 5.2 %copy.42 = f32[4,2,32,256]{3,2,1,0:T(8,128)S(1)} copy(f32[4,2,32,256]{0,3,2,1:T(8,128)} %bitcast.137) | data formatting | bytes 524288 | tf_op jit(solution)/shard_map/reshape | solution.py:32
  226.9 4.7 %copy.43 = f32[4,2,32,256]{0,3,2,1:T(8,128)} copy(f32[4,2,32,256]{3,2,1,0:T(8,128)S(1)} %slice.593) | data formatting | bytes 524288 | tf_op jit(solution)/shard_map/slice | solution.py:83
  231.7 5.6 %scatter_custom_fusion.7 = f32[4,16384]{0,1:T(8,128)} fusion(s32[64]{0:T(128)S(1)} %get-tuple-element.14, f32[]{:T(128)} %constant.71.clone.1, f32[]{:T(128)} %constant.79.clone.1, f32[64]{0:T(128)S(1)} %copy-done.18, pred[64]{0:T(512)(128)(4,1)S(1)} %get-tuple-element.13, f32[4,16384]{0,1:T(8,128)} %bitcast.124, s32[1024]{0:T(1024)S(1)} %pad_clamp_fusion), kind=kCustom, calls=%fused_computation.15 | custom fusion | flops 768 | bytes 529416 | tf_op jit(solution)/shard_map/scatter-add | solution.py:32
  237.3 5.3 %copy.44 = f32[4,2,32,256]{3,2,1,0:T(8,128)S(1)} copy(f32[4,2,32,256]{0,3,2,1:T(8,128)} %bitcast.125) | data formatting | bytes 524288 | tf_op jit(solution)/shard_map/reshape | solution.py:32
  244.0 45.1 %all-gather.4.cloned.1.call-done = f32[4,4,16384]{2,1,0:T(4,128)} async-done(((f32[1,4,16384]{2,1,0:T(4,128)}), f32[4,4,16384]{2,1,0:T(4,128)}) %all-gather.4.cloned.1.call-update) | async-done | bytes 1048592 | tf_op jit(solution)/shard_map/all_gather | solution.py:97
  292.1 51.3 %all-gather = f32[1024,16]{1,0:T(8,128)S(1)} all-gather(f32[16,16]{1,0:T(8,128)S(1)} %fusion.185), channel_id=2, replica_groups=mesh['probe'=4,'space'=64] {'space'}, dimensions={0}, use_global_device_ids=true | all-gather | bytes 66560 | tf_op jit(solution)/shard_map/all_gather | solution.py:98
  (166 shorter events, 81.1 us)
Async XLA Ops:
  7.2 40.4 %copy-start = (f32[2,32,256]{2,1,0:T(8,128)S(1)}, f32[2,32,256]{2,1,0:T(8,128)}, u32[]{:S(2)}) copy-start(f32[2,32,256]{2,1,0:T(8,128)} %param.10) | copy-start | bytes 196612
  7.2 41.0 %copy-start.1 = (f32[4,2,32,256]{3,2,1,0:T(8,128)S(1)}, f32[4,2,32,256]{3,2,1,0:T(8,128)}, u32[]{:S(2)}) copy-start(f32[4,2,32,256]{3,2,1,0:T(8,128)} %param.11) | copy-start | bytes 786436
  7.2 281.8 %all-gather.4.cloned.1.call-start = ((), (), s32[]{:S(2)}) async-start(), calls=%async_computation | async-start | bytes 1310720 | tf_op jit(solution)/shard_map/all_gather | solution.py:97
  15.6 3.1 collective-permute-start.1
  17.4 5.0 %collective-permute-start = (f32[5,1,32,256]{3,2,1,0:T(8,128)S(1)}, f32[5,1,32,256]{3,2,1,0:T(8,128)S(1)}, u32[]{:S(2)}, u32[]{:S(2)}) collective-permute-start(f32[5,1,32,256]{3,2,1,0:T(8,128)S(1)} %get-tuple-element.50), channel_id=1, source_target_pairs={{1,0},{2,1},{3,2},{4,3},{5,4},{6,5},{7,6},{8,7},{9,8},{10,9},{11,1... | collective-permute-start | bytes 491528 | tf_op jit(solution)/shard_map/ppermute | solution.py:15
  25.6 7.1 %collective-permute-start.3 = (f32[5,1,32,256]{3,2,1,0:T(8,128)S(1)}, f32[5,1,32,256]{3,2,1,0:T(8,128)S(1)}, u32[]{:S(2)}, u32[]{:S(2)}) collective-permute-start(f32[5,1,32,256]{3,2,1,0:T(8,128)S(1)} %get-tuple-element.29), channel_id=1, source_target_pairs={{0,1},{1,2},{2,3},{3,4},{4,5},{5,6},{6,7},{7,8},{8,9},{9,10},{10,1... | collective-permute-start | bytes 491528 | tf_op jit(solution)/shard_map/ppermute | solution.py:12
  31.3 3.3 collective-permute-start.2
  38.5 6.9 %collective-permute-start.5 = (f32[5,1,32,256]{3,2,1,0:T(8,128)S(1)}, f32[5,1,32,256]{3,2,1,0:T(8,128)S(1)}, u32[]{:S(2)}, u32[]{:S(2)}) collective-permute-start(f32[5,1,32,256]{3,2,1,0:T(8,128)S(1)} %get-tuple-element.27), channel_id=1, source_target_pairs={{0,1},{1,2},{2,3},{3,4},{4,5},{5,6},{6,7},{7,8},{8,9},{9,10},{10,1... | collective-permute-start | bytes 491528 | tf_op jit(solution)/shard_map/ppermute | solution.py:12
  44.0 3.3 collective-permute-start.4
  45.4 44.6 %copy-start.19 = (s32[64]{0:T(128)S(1)}, s32[64]{0:T(128)}, u32[]{:S(2)}) copy-start(s32[64]{0:T(128)} %param.16) | copy-start | bytes 772
  48.6 6.9 %collective-permute-start.7 = (f32[5,1,32,256]{3,2,1,0:T(8,128)S(1)}, f32[5,1,32,256]{3,2,1,0:T(8,128)S(1)}, u32[]{:S(2)}, u32[]{:S(2)}) collective-permute-start(f32[5,1,32,256]{3,2,1,0:T(8,128)S(1)} %get-tuple-element.25), channel_id=1, source_target_pairs={{0,1},{1,2},{2,3},{3,4},{4,5},{5,6},{6,7},{7,8},{8,9},{9,10},{10,1... | collective-permute-start | bytes 491528 | tf_op jit(solution)/shard_map/ppermute | solution.py:12
  54.1 3.3 collective-permute-start.6
  58.6 9.3 %collective-permute-start.9 = (f32[5,1,32,256]{3,2,1,0:T(8,128)S(1)}, f32[5,1,32,256]{3,2,1,0:T(8,128)S(1)}, u32[]{:S(2)}, u32[]{:S(2)}) collective-permute-start(f32[5,1,32,256]{3,2,1,0:T(8,128)S(1)} %get-tuple-element.23), channel_id=1, source_target_pairs={{0,1},{1,2},{2,3},{3,4},{4,5},{5,6},{6,7},{7,8},{8,9},{9,10},{10,1... | collective-permute-start | bytes 491528 | tf_op jit(solution)/shard_map/ppermute | solution.py:12
  66.6 3.3 collective-permute-start.8
  71.2 7.8 %collective-permute-start.11 = (f32[5,1,32,256]{3,2,1,0:T(8,128)S(1)}, f32[5,1,32,256]{3,2,1,0:T(8,128)S(1)}, u32[]{:S(2)}, u32[]{:S(2)}) collective-permute-start(f32[5,1,32,256]{3,2,1,0:T(8,128)S(1)} %get-tuple-element.21), channel_id=1, source_target_pairs={{0,1},{1,2},{2,3},{3,4},{4,5},{5,6},{6,7},{7,8},{8,9},{9,10},{10,1... | collective-permute-start | bytes 491528 | tf_op jit(solution)/shard_map/ppermute | solution.py:12
  77.6 3.3 collective-permute-start.10
  78.9 18.2 %copy-start.18 = (f32[64]{0:T(128)S(1)}, f32[64]{0:T(128)}, u32[]{:S(2)}) copy-start(f32[64]{0:T(128)} %param.17) | copy-start | bytes 772
  82.2 7.9 %collective-permute-start.13 = (f32[5,1,32,256]{3,2,1,0:T(8,128)S(1)}, f32[5,1,32,256]{3,2,1,0:T(8,128)S(1)}, u32[]{:S(2)}, u32[]{:S(2)}) collective-permute-start(f32[5,1,32,256]{3,2,1,0:T(8,128)S(1)} %get-tuple-element.19), channel_id=1, source_target_pairs={{0,1},{1,2},{2,3},{3,4},{4,5},{5,6},{6,7},{7,8},{8,9},{9,10},{10,1... | collective-permute-start | bytes 491528 | tf_op jit(solution)/shard_map/ppermute | solution.py:12
  88.7 3.3 collective-permute-start.12
  108.0 23.3 %collective-permute-start.15 = (f32[4,1,32,256]{3,2,1,0:T(8,128)S(1)}, f32[4,1,32,256]{3,2,1,0:T(8,128)S(1)}, u32[]{:S(2)}, u32[]{:S(2)}) collective-permute-start(f32[4,1,32,256]{3,2,1,0:T(8,128)S(1)} %get-tuple-element.41), channel_id=1, source_target_pairs={{0,1},{1,2},{2,3},{3,4},{4,5},{5,6},{6,7},{7,8},{8,9},{9,10},{10,1... | collective-permute-start | bytes 393224 | tf_op jit(solution)/shard_map/ppermute | solution.py:12
  114.5 16.9 %collective-permute-start.14 = (f32[4,1,32,256]{3,2,1,0:T(8,128)S(1)}, f32[4,1,32,256]{3,2,1,0:T(8,128)S(1)}, u32[]{:S(2)}, u32[]{:S(2)}) collective-permute-start(f32[4,1,32,256]{3,2,1,0:T(8,128)S(1)} %get-tuple-element.40), channel_id=1, source_target_pairs={{1,0},{2,1},{3,2},{4,3},{5,4},{6,5},{7,6},{8,7},{9,8},{10,9},{11,1... | collective-permute-start | bytes 393224 | tf_op jit(solution)/shard_map/ppermute | solution.py:15
  131.6 20.1 %collective-permute-start.17 = (f32[4,1,32,256]{3,2,1,0:T(8,128)S(1)}, f32[4,1,32,256]{3,2,1,0:T(8,128)S(1)}, u32[]{:S(2)}, u32[]{:S(2)}) collective-permute-start(f32[4,1,32,256]{3,2,1,0:T(8,128)S(1)} %get-tuple-element.39), channel_id=1, source_target_pairs={{0,1},{1,2},{2,3},{3,4},{4,5},{5,6},{6,7},{7,8},{8,9},{9,10},{10,1... | collective-permute-start | bytes 393224 | tf_op jit(solution)/shard_map/ppermute | solution.py:12
  134.6 17.0 %collective-permute-start.16 = (f32[4,1,32,256]{3,2,1,0:T(8,128)S(1)}, f32[4,1,32,256]{3,2,1,0:T(8,128)S(1)}, u32[]{:S(2)}, u32[]{:S(2)}) collective-permute-start(f32[4,1,32,256]{3,2,1,0:T(8,128)S(1)} %get-tuple-element.38), channel_id=1, source_target_pairs={{1,0},{2,1},{3,2},{4,3},{5,4},{6,5},{7,6},{8,7},{9,8},{10,9},{11,1... | collective-permute-start | bytes 393224 | tf_op jit(solution)/shard_map/ppermute | solution.py:15
  151.9 22.5 %collective-permute-start.19 = (f32[4,1,32,256]{3,2,1,0:T(8,128)S(1)}, f32[4,1,32,256]{3,2,1,0:T(8,128)}, u32[]{:S(2)}, u32[]{:S(2)}) collective-permute-start(f32[4,1,32,256]{3,2,1,0:T(8,128)S(1)} %get-tuple-element.37), channel_id=1, source_target_pairs={{0,1},{1,2},{2,3},{3,4},{4,5},{5,6},{6,7},{7,8},{8,9},{9,10},{10,1... | collective-permute-start | bytes 393224 | tf_op jit(solution)/shard_map/ppermute | solution.py:12
  157.6 16.9 %collective-permute-start.18 = (f32[4,1,32,256]{3,2,1,0:T(8,128)S(1)}, f32[4,1,32,256]{3,2,1,0:T(8,128)}, u32[]{:S(2)}, u32[]{:S(2)}) collective-permute-start(f32[4,1,32,256]{3,2,1,0:T(8,128)S(1)} %get-tuple-element.36), channel_id=1, source_target_pairs={{1,0},{2,1},{3,2},{4,3},{5,4},{6,5},{7,6},{8,7},{9,8},{10,9},{11,1... | collective-permute-start | bytes 393224 | tf_op jit(solution)/shard_map/ppermute | solution.py:15
  175.7 21.1 %collective-permute-start.21 = (f32[4,1,32,256]{3,2,1,0:T(8,128)S(1)}, f32[4,1,32,256]{3,2,1,0:T(8,128)}, u32[]{:S(2)}, u32[]{:S(2)}) collective-permute-start(f32[4,1,32,256]{3,2,1,0:T(8,128)S(1)} %get-tuple-element.35), channel_id=1, source_target_pairs={{0,1},{1,2},{2,3},{3,4},{4,5},{5,6},{6,7},{7,8},{8,9},{9,10},{10,1... | collective-permute-start | bytes 393224 | tf_op jit(solution)/shard_map/ppermute | solution.py:12
  180.0 16.9 %collective-permute-start.20 = (f32[4,1,32,256]{3,2,1,0:T(8,128)S(1)}, f32[4,1,32,256]{3,2,1,0:T(8,128)}, u32[]{:S(2)}, u32[]{:S(2)}) collective-permute-start(f32[4,1,32,256]{3,2,1,0:T(8,128)S(1)} %get-tuple-element.34), channel_id=1, source_target_pairs={{1,0},{2,1},{3,2},{4,3},{5,4},{6,5},{7,6},{8,7},{9,8},{10,9},{11,1... | collective-permute-start | bytes 393224 | tf_op jit(solution)/shard_map/ppermute | solution.py:15
  198.1 20.5 %collective-permute-start.23 = (f32[4,1,32,256]{3,2,1,0:T(8,128)S(1)}, f32[4,1,32,256]{3,2,1,0:T(8,128)S(1)}, u32[]{:S(2)}, u32[]{:S(2)}) collective-permute-start(f32[4,1,32,256]{3,2,1,0:T(8,128)S(1)} %get-tuple-element.33), channel_id=1, source_target_pairs={{0,1},{1,2},{2,3},{3,4},{4,5},{5,6},{6,7},{7,8},{8,9},{9,10},{10,1... | collective-permute-start | bytes 393224 | tf_op jit(solution)/shard_map/ppermute | solution.py:12
  201.7 16.9 %collective-permute-start.22 = (f32[4,1,32,256]{3,2,1,0:T(8,128)S(1)}, f32[4,1,32,256]{3,2,1,0:T(8,128)S(1)}, u32[]{:S(2)}, u32[]{:S(2)}) collective-permute-start(f32[4,1,32,256]{3,2,1,0:T(8,128)S(1)} %get-tuple-element.32), channel_id=1, source_target_pairs={{1,0},{2,1},{3,2},{4,3},{5,4},{6,5},{7,6},{8,7},{9,8},{10,9},{11,1... | collective-permute-start | bytes 393224 | tf_op jit(solution)/shard_map/ppermute | solution.py:15
  221.1 21.5 %collective-permute-start.25 = (f32[4,1,32,256]{3,2,1,0:T(8,128)S(1)}, f32[4,1,32,256]{3,2,1,0:T(8,128)S(1)}, u32[]{:S(2)}, u32[]{:S(2)}) collective-permute-start(f32[4,1,32,256]{3,2,1,0:T(8,128)S(1)} %get-tuple-element.31), channel_id=1, source_target_pairs={{0,1},{1,2},{2,3},{3,4},{4,5},{5,6},{6,7},{7,8},{8,9},{9,10},{10,1... | collective-permute-start | bytes 393224 | tf_op jit(solution)/shard_map/ppermute | solution.py:12
  225.4 17.2 %collective-permute-start.24 = (f32[4,1,32,256]{3,2,1,0:T(8,128)S(1)}, f32[4,1,32,256]{3,2,1,0:T(8,128)S(1)}, u32[]{:S(2)}, u32[]{:S(2)}) collective-permute-start(f32[4,1,32,256]{3,2,1,0:T(8,128)S(1)} %get-tuple-element.30), channel_id=1, source_target_pairs={{1,0},{2,1},{3,2},{4,3},{5,4},{6,5},{7,6},{8,7},{9,8},{10,9},{11,1... | collective-permute-start | bytes 393224 | tf_op jit(solution)/shard_map/ppermute | solution.py:15
  243.1 106.4 %copy-start.2 = (f32[4,2,32,256]{3,2,1,0:T(8,128)}, f32[4,2,32,256]{3,2,1,0:T(8,128)S(1)}, u32[]{:S(2)}) copy-start(f32[4,2,32,256]{3,2,1,0:T(8,128)S(1)} %fusion.103) | copy-start | bytes 786436
  (15 other events, 52.8 us)
Sparse Core Ops, SparseCore 0:
  244.1 44.8 all-gather.3
